TPU v7x, 256 devices: a whole 4x4x8 slice. The times are simulated.
256 devices in a mesh: dp: 8 (over z), seq: 32 (over y, x, core).
Axes of the slice: x: 4, y: 4, z: 8, core: 2. Of those that a mesh axis runs over, the one named last changes fastest.
Arguments:
- embeddings: bfloat16 [8, 16384, 512], P('dp', 'seq'), may hold values from -6 to 6
- user_ids: int32 [8, 16384], P('dp', 'seq'), may hold values from 0 to 63, never falling along the last dimension, each value on 1 to 512 neighbouring positions
- time_gaps: int32 [8, 16384], P('dp', 'seq'), may hold values from 0 to 16
- proj_weight: bfloat16 [512, 2048], replicated, may hold values from -0.25 to 0.25
- out_weight: bfloat16 [512, 512], replicated, may hold values from -0.25 to 0.25
- frequencies: float32 [64], replicated, may hold values from 0.001 to 0.1
- time_mix: float32 [4, 64], replicated, may hold values from -0.9 to 0.9
- cotangent: bfloat16 [8, 16384, 512], P('dp', 'seq'), may hold values from -6 to 6
Outputs:
- layer_out: bfloat16 [8, 16384, 512], P('dp', 'seq')
- grad_input: bfloat16 [8, 16384, 512], P('dp', 'seq')
- grad_proj: float32 [512, 2048], P('seq')
- grad_out_weight: float32 [512, 512], P('seq')
- grad_time_mix: float32 [4, 64], replicated
Inputs may be any that keep to these rules, and one draw needn't show every extreme that they name: `user_ids`: within a stream the ids never fall, so each user's events are consecutive; a user holds at most 512 events, and some user holds exactly that many.
All inputs are finite; a program needn't handle non-finite values.
Results may differ from a plain program's by a relative error of at most 0.019.
Values may be sent and summed in bfloat16 or wider, within the bound.
A program may use at most 64 MiB of HBM per device.

v0:
```python
import jax
import jax.numpy as jnp
from jax import lax
from jax.sharding import PartitionSpec as P

BLOCK = 512
REACH = 1
EPSILON = 1e-05
HIGH = lax.Precision.HIGHEST


def entering(value, axis, join, neutral):
    count, mine = (lax.axis_size(axis), lax.axis_index(axis))
    pieces = jax.tree.map(lambda part: lax.all_gather(part, axis), value)
    total = jax.tree.map(
        lambda part, zero: jnp.full_like(part, 0) + jnp.asarray(zero, part.dtype), value, neutral
    )

    def turn(position, total):
        longer = join(total, jax.tree.map(lambda part: part[position], pieces))
        return jax.tree.map(lambda new, old: jnp.where(position < mine, new, old), longer, total)

    return lax.fori_loop(0, count - 1, turn, total)


def shifted(array, axis, by):
    length = lax.axis_size(axis)
    pairs = [(i, i + by) for i in range(length) if 0 <= i + by < length]
    return lax.ppermute(array, axis, pairs)


def silu_slope(value):
    sigma = jax.nn.sigmoid(value)
    return sigma * (1.0 + value * (1.0 - sigma))


def run_times(users, gaps):
    count = users.shape[0]
    running = jnp.cumsum(gaps)
    position = jnp.arange(count, dtype=jnp.int32)
    before = jnp.concatenate([users[:1] - 1, users[:-1]])
    opening = jnp.where(users != before, position, 0)
    first = lax.cummax(opening, axis=0)
    return running - (running[first] - gaps[first])


def combine(earlier, later):
    valid_a, user_a, total_a, whole_a = earlier
    valid_b, user_b, total_b, whole_b = later
    both = (valid_a == 1) & (valid_b == 1)
    has_later = valid_b == 1
    same = user_a == user_b
    joined = jnp.where((whole_b == 1) & same, total_a + total_b, total_b)
    merged_whole = jnp.where((whole_a == 1) & (whole_b == 1) & same, 1, 0)
    return (
        jnp.maximum(valid_a, valid_b).astype(jnp.int32),
        jnp.where(has_later, user_b, user_a).astype(jnp.int32),
        jnp.where(both, joined, jnp.where(has_later, total_b, total_a)).astype(jnp.int32),
        jnp.where(both, merged_whole, jnp.where(has_later, whole_b, whole_a)).astype(jnp.int32),
    )


def time_features(times, frequencies, time_mix):
    angles = times.astype(jnp.float32)[:, None] * frequencies[None, :]
    cosines = jnp.cos(angles)
    sines = jnp.sin(angles)
    key_time = jnp.concatenate([cosines, sines], 1).astype(jnp.bfloat16)
    query_time = jnp.concatenate(
        [cosines[:, None, :] * time_mix[None], sines[:, None, :] * time_mix[None]], 2
    ).astype(jnp.bfloat16)
    return (cosines, sines, key_time, query_time)


def project(events, proj_weight):
    values_wide = events.astype(jnp.float32)
    scale_in = lax.rsqrt(jnp.mean(values_wide * values_wide, -1, keepdims=True) + EPSILON)
    unit_rows = values_wide * scale_in
    normed = unit_rows.astype(jnp.bfloat16)
    preact = jnp.dot(normed, proj_weight, preferred_element_type=jnp.float32)
    hidden = jax.nn.silu(preact).astype(jnp.bfloat16)
    return (scale_in, unit_rows, normed, preact, hidden)


def pair_scores(query, query_time, keys, key_time):
    inverse = query.shape[-1] ** (-0.5)
    return jnp.einsum(
        "qhd,khd->hqk", query, keys, preferred_element_type=jnp.float32
    ) * inverse + jnp.einsum(
        "qhf,kf->hqk", query_time, key_time, preferred_element_type=jnp.float32
    )


def pair_mask(query_user, query_pos, key_user, key_pos):
    return (
        (key_user[None, :] == query_user[:, None])
        & (key_pos[None, :] <= query_pos[:, None])
        & (key_pos[None, :] >= 0)
    )


def forward_pair(operands):
    query, query_time, query_user, query_pos, keys, values, key_time, key_user, key_pos = operands
    mask = pair_mask(query_user, query_pos, key_user, key_pos)
    scores = pair_scores(query, query_time, keys, key_time)
    weights = jnp.where(mask[None], jax.nn.silu(scores), 0.0).astype(jnp.bfloat16)
    return jnp.einsum("hqk,khd->qhd", weights, values, preferred_element_type=jnp.float32)


def forward_none(operands):
    return jnp.zeros(operands[0].shape, jnp.float32)


def backward_pair(operands):
    (
        query,
        query_time,
        query_user,
        query_pos,
        grad_tile,
        keys,
        values,
        key_time,
        key_user,
        key_pos,
    ) = operands
    inverse = query.shape[-1] ** (-0.5)
    mask = pair_mask(query_user, query_pos, key_user, key_pos)
    scores = pair_scores(query, query_time, keys, key_time)
    weights = jnp.where(mask[None], jax.nn.silu(scores), 0.0).astype(jnp.bfloat16)
    grad_weights = jnp.einsum("qhd,khd->hqk", grad_tile, values, preferred_element_type=jnp.float32)
    grad_scores = jnp.where(mask[None], grad_weights * silu_slope(scores), 0.0).astype(jnp.bfloat16)
    value_part = jnp.einsum("hqk,qhd->khd", weights, grad_tile, preferred_element_type=jnp.float32)
    key_part = (
        jnp.einsum("hqk,qhd->khd", grad_scores, query, preferred_element_type=jnp.float32) * inverse
    )
    query_part = (
        jnp.einsum("hqk,khd->qhd", grad_scores, keys, preferred_element_type=jnp.float32) * inverse
    )
    qtime_part = jnp.einsum(
        "hqk,kf->qhf", grad_scores, key_time, preferred_element_type=jnp.float32
    )
    return (query_part, qtime_part, key_part, value_part)


def backward_none(operands):
    return (
        jnp.zeros(operands[0].shape, jnp.float32),
        jnp.zeros(operands[1].shape, jnp.float32),
        jnp.zeros(operands[5].shape, jnp.float32),
        jnp.zeros(operands[6].shape, jnp.float32),
    )


def body(
    embeddings, user_ids, time_gaps, proj_weight, out_weight, frequencies, time_mix, cotangent
):
    events = embeddings[0]
    users = user_ids[0]
    gaps = time_gaps[0]
    upstream = cotangent[0]
    count = events.shape[0]
    model_width = events.shape[1]
    heads = time_mix.shape[0]
    head_size = model_width // heads
    freq_count = frequencies.shape[0]
    device = lax.axis_index("seq")
    seq_devices = lax.axis_size("seq")
    local_times = run_times(users, gaps)
    summary = (
        jnp.ones((1,), jnp.int32),
        users[-1:],
        local_times[-1:],
        (users[:1] == users[-1:]).astype(jnp.int32),
    )
    identity = (
        jnp.zeros((1,), jnp.int32),
        jnp.zeros((1,), jnp.int32),
        jnp.zeros((1,), jnp.int32),
        jnp.zeros((1,), jnp.int32),
    )
    carried = entering(summary, "seq", combine, identity)
    times = (
        local_times + jnp.where((carried[0] == 1) & (users == carried[1]), carried[2], 0)
    ).astype(jnp.int32)
    cosines, sines, key_time, query_time = time_features(times, frequencies, time_mix)
    scale_in, unit_rows, normed, preact, hidden = project(events, proj_weight)
    gate_part = hidden[:, :model_width]
    value_flat = hidden[:, model_width : 2 * model_width]
    query_flat = hidden[:, 2 * model_width : 3 * model_width]
    key_flat = hidden[:, 3 * model_width :]
    user_marks = users.astype(jnp.bfloat16)
    positions = device * count + jnp.arange(count, dtype=jnp.int32)
    sources = []
    distance = 1
    received = shifted((key_flat, value_flat, key_time, user_marks), "seq", distance)
    sources.append(
        (received[0], received[1], received[2], received[3], positions - distance * count)
    )
    sources.append((key_flat, value_flat, key_time, user_marks, positions))

    def head_tile(flat):
        return flat.reshape(BLOCK, heads, head_size)

    def key_operands(source_index):
        keys, values, times_part, marks, places = sources[source_index]
        return (head_tile(keys), head_tile(values), times_part, marks, places)

    def query_operands():
        return (head_tile(query_flat), query_time, user_marks, positions)

    def candidates():
        listed = []
        tile_index = 0
        listed.append((0, tile_index))
        tile_index = 0
        listed.append((REACH, tile_index))
        return listed

    def is_live(query_part, key_part):
        return (key_part[3][-1] >= query_part[2][0]) & (key_part[4][-1] >= 0)

    query_part = query_operands()
    total = jnp.zeros((BLOCK, heads, head_size), jnp.float32)
    for pair in candidates():
        key_part = key_operands(pair[0])
        total = total + lax.cond(
            is_live(query_part, key_part), forward_pair, forward_none, query_part + key_part
        )
    attended = total.reshape(count, model_width)
    scale_mid = lax.rsqrt(jnp.mean(attended * attended, -1, keepdims=True) + EPSILON)
    normed_mid = attended * scale_mid
    gate_wide = gate_part.astype(jnp.float32)
    gated = (normed_mid * gate_wide).astype(jnp.bfloat16)
    layer_out = (
        events.astype(jnp.float32) + jnp.dot(gated, out_weight, preferred_element_type=jnp.float32)
    ).astype(jnp.bfloat16)
    grad_gated = jnp.einsum("ef,df->ed", upstream, out_weight, preferred_element_type=jnp.float32)
    grad_gate = grad_gated * normed_mid
    grad_mid = grad_gated * gate_wide
    grad_attended = (
        scale_mid * (grad_mid - normed_mid * jnp.mean(grad_mid * normed_mid, -1, keepdims=True))
    ).astype(jnp.bfloat16)
    key_grads = {}
    query_part = query_operands()
    grad_tile = head_tile(grad_attended)
    grad_query = jnp.zeros((BLOCK, heads, head_size), jnp.float32)
    grad_qtime = jnp.zeros((BLOCK, heads, 2 * freq_count), jnp.float32)
    for pair in candidates():
        key_part = key_operands(pair[0])
        result = lax.cond(
            is_live(query_part, key_part),
            backward_pair,
            backward_none,
            query_part + (grad_tile,) + key_part,
        )
        grad_query = grad_query + result[0]
        grad_qtime = grad_qtime + result[1]
        key_grads[pair] = (result[2], result[3])

    def source_grads(source_index):
        keys_part = key_grads[source_index, 0][0]
        values_part = key_grads[source_index, 0][1]
        return (keys_part.reshape(count, model_width), values_part.reshape(count, model_width))

    grad_keys_flat, grad_values_flat = source_grads(REACH)
    distance = 1
    partial_keys, partial_values = source_grads(distance - 1)
    returned = (
        shifted(partial_keys.astype(jnp.bfloat16), "seq", -distance).astype(partial_keys.dtype),
        shifted(partial_values.astype(jnp.bfloat16), "seq", -distance).astype(partial_values.dtype),
    )
    grad_keys_flat = grad_keys_flat + returned[0]
    grad_values_flat = grad_values_flat + returned[1]
    grad_query_flat = grad_query.reshape(count, model_width)
    grad_act = jnp.concatenate([grad_gate, grad_values_flat, grad_query_flat, grad_keys_flat], 1)
    grad_pre = (grad_act * silu_slope(preact)).astype(jnp.bfloat16)
    grad_normed = jnp.einsum("ef,df->ed", grad_pre, proj_weight, preferred_element_type=jnp.float32)
    grad_input = (
        upstream.astype(jnp.float32)
        + scale_in
        * (grad_normed - unit_rows * jnp.mean(grad_normed * unit_rows, -1, keepdims=True))
    ).astype(jnp.bfloat16)
    proj_part = jnp.einsum("ed,ef->df", normed, grad_pre, preferred_element_type=jnp.float32)
    out_part = jnp.einsum("ed,ef->df", gated, upstream, preferred_element_type=jnp.float32)
    whole = lax.psum(jnp.concatenate([proj_part, out_part], 1).astype(jnp.bfloat16), "dp")
    shard = lax.psum_scatter(whole, "seq", scatter_dimension=0, tiled=True).astype(jnp.float32)
    grad_mix = jnp.einsum(
        "ehf,ef->hf", grad_qtime[:, :, :freq_count], cosines, precision=HIGH
    ) + jnp.einsum("ehf,ef->hf", grad_qtime[:, :, freq_count:], sines, precision=HIGH)
    grad_mix = lax.psum(grad_mix, ("dp", "seq"))
    factor = float(lax.axis_size("dp") * seq_devices * count) ** (-0.5)
    grad_proj = shard[:, : 4 * model_width] * factor
    grad_out_weight = shard[:, 4 * model_width :] * factor
    return (layer_out[None], grad_input[None], grad_proj, grad_out_weight, grad_mix * factor)


def solution(mesh):
    return jax.shard_map(
        body,
        mesh=mesh,
        in_specs=(
            P("dp", "seq", None),
            P("dp", "seq"),
            P("dp", "seq"),
            P(),
            P(),
            P(),
            P(),
            P("dp", "seq", None),
        ),
        out_specs=(P("dp", "seq", None), P("dp", "seq", None), P("seq", None), P("seq", None), P()),
        check_vma=False,
    )
```

profile of v0, /device:TPU:32, one launch (start us, length us, event | category | flops | bytes accessed | tf_op | source)
XLA Modules:
  0.0 555.3 jit_solution(1448338192975510792)
XLA Ops:
  8.1 2.3 collective-permute-start
  16.4 3.6 gather_fusion.1
  20.0 3.5 gather_fusion
  27.7 16.6 %all-reduce.4 = (s32[32]{0:T(128)S(1)}, s32[32]{0:T(128)S(1)}, s32[32]{0:T(128)S(1)}, s32[32]{0:T(128)S(1)}) all-reduce(s32[32]{0:T(128)S(1)} %dynamic-update-slice, s32[32]{0:T(128)S(1)} %bitcast_dynamic-update-slice_fusion.1, s32[32]{0:T(128)S(1)} %bitcast_dynamic-update-slice_fusion, ...), channel_id=1, replica_groups=mesh['dp'=8,'seq'=32] {'seq'}, use_global_device_ids=true, to_apply=%add | all-reduce | flops 128 | bytes 1024
  44.3 217.0 %while.17 = (s32[]{:T(128)}, s32[1]{0:T(128)}, s32[1]{0:T(128)}, s32[1]{0:T(128)}, s32[]{:T(128)}, /*index=5*/s32[32,1]{0,1:T(1,128)S(1)}, s32[32,1]{0,1:T(1,128...) while((s32[]{:T(128)}, s32[1]{0:T(128)}, s32[1]{0:T(128)}, s32[1]{0:T(128)}, ...), condition=%wide.region_6.7_spmd, body=%wide.region_5.6_spmd.sunk | while | flops 18 | bytes 315 | solution.py:23
  265.4 3.6 multiply_convert_fusion
  271.6 3.8 collective-permute-start.3
  275.4 2.1 collective-permute-start.1
  279.5 2.0 reshape.538
  281.5 2.0 reshape.537
  288.4 10.0 %conditional.5 = (f32[512,4,128]{2,0,1:T(8,128)}) conditional(s32[]{:T(128)} %bitcast.54, () %tuple.57, (bf16[512]{0:T(512)(128)(2,1)S(1)}, s32[512]{0:T(512)S(1)}, bf16[512,4,128]{2,1,0:T(4,128)(2,1)S(1)}, bf16[512,4,128]{2,1,0:T(4,128)(2,1)}, bf16[512,128]{1,0:T(8,128)(2,1)S(1)}, /*index=5*/bf16[512,4,128]{2,0,1:T(8,128)(2,1)S(1)}, ...), branch_computations={%region_9.10_spmd, %region_10.11_spmd} | conditional | flops 815268352 | bytes 12195848 | solution.py:226
  289.5 3.7 fusion.14
  293.2 5.2 fusion.12
  301.0 1.9 reshape.536
  303.0 2.0 reshape.532
  307.7 2.0 multiply_reduce_fusion
  309.7 2.8 multiply_convert_fusion.1
  312.5 2.0 reshape.540
  319.1 29.8 %conditional.6 = (f32[512,4,128]{2,0,1:T(8,128)}, f32[512,4,128]{2,0,1:T(8,128)}, f32[512,512]{1,0:T(8,128)}, f32[512,512]{1,0:T(8,128)}) conditional(s32[]{:T(128)} %bitcast.54, () %tuple.59, (bf16[512]{0:T(512)(128)(2,1)S(1)}, s32[512]{0:T(512)S(1)}, bf16[512,4,128]{2,1,0:T(4,128)(2,1)}, bf16[512,4,128]{2,1,0:T(4,128)(2,1)}, ...), branch_computations={%region_13.14_spmd, %region_14.15_spmd} | conditional | flops 1900020224 | bytes 65018056 | solution.py:250
  322.8 2.1 fusion.26
  325.9 2.3 fusion.22
  328.3 4.3 select_convert_fusion.3
  332.6 2.5 copy.107
  335.1 3.6 fusion.23
  338.7 2.5 copy.53
  341.2 2.6 copy.109
  343.8 3.4 fusion.24
  364.6 101.5 %psum.15 = f32[4,64]{1,0:T(4,128)S(1)} all-reduce(f32[4,64]{1,0:T(4,128)S(1)} %add_bitcast_fusion.3), channel_id=1, replica_groups=mesh['dp'=8,'seq'=32] {'dp','seq'}, use_global_device_ids=true, to_apply=%region_20.21 | all-reduce | flops 256 | bytes 2048 | tf_op jit(solution)/shard_map/psum | solution.py:290
  466.1 2.3 fusion.54
  469.0 3.9 fusion.56
  473.0 2.3 fusion.67
  475.3 71.0 %all-reduce.7.cloned.1.call-done = bf16[16,2560]{1,0:T(8,128)(2,1)} async-done(((bf16[16,2560]{1,0:T(8,128)(2,1)}), bf16[16,2560]{1,0:T(8,128)(2,1)}) %all-reduce.7.cloned.1.call-update) | async-done | bytes 81936 | tf_op jit(solution)/shard_map/psum | solution.py:285
  (224 shorter events, 115.3 us)
Async XLA Ops:
  7.2 258.2 %copy-start = (bf16[512,2048]{1,0:T(8,128)(2,1)S(1)}, bf16[512,2048]{1,0:T(8,128)(2,1)}, u32[]{:S(2)}) copy-start(bf16[512,2048]{1,0:T(8,128)(2,1)} %param.21) | copy-start | bytes 6291460
  7.2 16.4 %copy-start.23 = (u32[256]{0:T(256)S(1)}, u32[256]{0:T(256)}, u32[]{:S(2)}) copy-start(u32[256]{0:T(256)} %constant.130) | copy-start | bytes 3076
  7.2 254.1 %copy-start.20 = (s32[1,512]{1,0:T(1,128)S(1)}, s32[1,512]{1,0:T(1,128)}, u32[]{:S(2)}) copy-start(s32[1,512]{1,0:T(1,128)} %param.19) | copy-start | bytes 6148
  7.2 254.1 %copy-start.22 = (f32[64]{0:T(128)S(1)}, f32[64]{0:T(128)}, u32[]{:S(2)}) copy-start(f32[64]{0:T(128)} %param.23) | copy-start | bytes 772
  7.2 258.0 %copy-start.5 = (bf16[1,512,512]{2,1,0:T(8,128)(2,1)S(1)}, bf16[1,512,512]{2,1,0:T(8,128)(2,1)}, u32[]{:S(2)}) copy-start(bf16[1,512,512]{2,1,0:T(8,128)(2,1)} %param.18) | copy-start | bytes 1572868
  7.2 465.7 %reduce-scatter.2.cloned.1.call-start = ((), (), s32[]{:S(2)}) async-start(), calls=%async_computation.1 | async-start | bytes 2703360 | tf_op jit(solution)/shard_map/reduce_scatter | solution.py:286
  8.1 290.3 %collective-permute-start = (bf16[512]{0:T(512)(128)(2,1)S(1)}, bf16[512]{0:T(512)(128)(2,1)}, u32[]{:S(2)}, u32[]{:S(2)}) collective-permute-start(bf16[512]{0:T(512)(128)(2,1)S(1)} %convert_reduce_fusion), channel_id=1, source_target_pairs={{0,1},{1,2},{2,3},{3,4},{4,5},{5,6},{6,7},{7,8},{8,9},{9,10},{10,1... | collective-permute-start | bytes 3080 | tf_op jit(solution)/shard_map/ppermute | solution.py:29
  263.3 41.7 %collective-permute-start.2 = (bf16[512,128]{1,0:T(8,128)(2,1)S(1)}, bf16[512,128]{1,0:T(8,128)(2,1)}, u32[]{:S(2)}, u32[]{:S(2)}) collective-permute-start(bf16[512,128]{1,0:T(8,128)(2,1)S(1)} %pad_maximum_fusion.2), channel_id=1, source_target_pairs={{0,1},{1,2},{2,3},{3,4},{4,5},{5,6},{6,7},{7,8},{8,9},{9,10},{10,1... | collective-permute-start | bytes 393224 | tf_op jit(solution)/shard_map/ppermute | solution.py:29
  265.4 12.1 %copy-start.21 = (f32[4,64]{1,0:T(4,128)S(1)}, f32[4,64]{1,0:T(4,128)}, u32[]{:S(2)}) copy-start(f32[4,64]{1,0:T(4,128)} %param.24) | copy-start | bytes 3076
  269.1 1.4 copy-start.11
  271.6 29.4 %collective-permute-start.3 = (bf16[512,512]{1,0:T(8,128)(2,1)}, bf16[512,512]{1,0:T(8,128)(2,1)}, u32[]{:S(2)}, u32[]{:S(2)}) collective-permute-start(bf16[512,512]{1,0:T(8,128)(2,1)} %get-tuple-element.395), channel_id=1, source_target_pairs={{0,1},{1,2},{2,3},{3,4},{4,5},{5,6},{6,7},{7,8},{8,9},{9,10},{10,1... | collective-permute-start | bytes 1572872 | tf_op jit(solution)/shard_map/ppermute | solution.py:29
  275.4 27.6 %collective-permute-start.1 = (bf16[512,512]{1,0:T(8,128)(2,1)}, bf16[512,512]{1,0:T(8,128)(2,1)}, u32[]{:S(2)}, u32[]{:S(2)}) collective-permute-start(bf16[512,512]{1,0:T(8,128)(2,1)} %get-tuple-element.396), channel_id=1, source_target_pairs={{0,1},{1,2},{2,3},{3,4},{4,5},{5,6},{6,7},{7,8},{8,9},{9,10},{10,1... | collective-permute-start | bytes 1572872 | tf_op jit(solution)/shard_map/ppermute | solution.py:29
  314.7 4.4 copy-start.7
  314.7 4.4 copy-start.8
  316.5 37.5 %collective-permute-start.5 = (bf16[512,512]{1,0:T(8,128)(2,1)}, bf16[512,512]{1,0:T(8,128)(2,1)}, u32[]{:S(2)}, u32[]{:S(2)}) collective-permute-start(bf16[512,512]{1,0:T(8,128)(2,1)} %copy_bitcast_fusion.1), channel_id=1, source_target_pairs={{1,0},{2,1},{3,2},{4,3},{5,4},{6,5},{7,6},{8,7},{9,8},{10,9},{11,1... | collective-permute-start | bytes 1572872 | tf_op jit(solution)/shard_map/ppermute | solution.py:29
  317.8 34.6 %collective-permute-start.4 = (bf16[512,512]{1,0:T(8,128)(2,1)}, bf16[512,512]{1,0:T(8,128)(2,1)}, u32[]{:S(2)}, u32[]{:S(2)}) collective-permute-start(bf16[512,512]{1,0:T(8,128)(2,1)} %copy_bitcast_fusion.2), channel_id=1, source_target_pairs={{1,0},{2,1},{3,2},{4,3},{5,4},{6,5},{7,6},{8,7},{9,8},{10,9},{11,1... | collective-permute-start | bytes 1572872 | tf_op jit(solution)/shard_map/ppermute | solution.py:29
  322.8 2.9 copy-start.18
  325.0 1.0 copy-start.19
  325.9 2.3 copy-start.16
  328.3 6.8 %copy-start.4 = (bf16[512,4,128]{0,2,1:T(8,128)(2,1)S(1)}, bf16[512,4,128]{0,2,1:T(8,128)(2,1)}, u32[]{:S(2)}) copy-start(bf16[512,4,128]{0,2,1:T(8,128)(2,1)} %copy.68) | copy-start | bytes 1572868 | tf_op jit(solution)/shard_map/cond
  335.1 8.6 %copy-start.2 = (bf16[512,4,128]{2,1,0:T(4,128)(2,1)S(1)}, bf16[512,4,128]{2,1,0:T(4,128)(2,1)}, u32[]{:S(2)}) copy-start(bf16[512,4,128]{2,1,0:T(4,128)(2,1)} %get-tuple-element.349) | copy-start | bytes 1572868 | tf_op jit(solution)/shard_map/cond
  343.8 3.4 copy-start.1
  350.6 4.9 copy-start.9
  350.6 4.9 copy-start.10
  355.6 2.9 copy-start.6
  357.1 1.3 copy-start.12
  361.5 104.6 %copy-start.15 = (bf16[512,512]{1,0:T(8,128)(2,1)S(1)}, bf16[512,512]{1,0:T(8,128)(2,1)}, u32[]{:S(2)}) copy-start(bf16[512,512]{1,0:T(8,128)(2,1)} %param.22) | copy-start | bytes 1572868
  361.6 184.7 %all-reduce.7.cloned.1.call-start = ((), (), s32[]{:S(2)}) async-start(), calls=%async_computation.2 | async-start | bytes 163840 | tf_op jit(solution)/shard_map/psum | solution.py:285
  468.4 4.6 copy-start.13
Sparse Core Ops, SparseCore 0:
  361.7 111.2 reduce-scatter.1
  475.3 70.9 all-reduce.6
where the time goes:
time: 559 us; the launch traced here: 555 us
  loops' own time  158 us (28%)
  blocking collectives  118 us (21%)
  local copies, waits for them, and re-layouts  81.7 us (15%)
  waiting for transfers between devices  71.1 us (13%)
  other arithmetic  51.5 us (9%)
  matrix products  42.1 us (8%)
  between operations  20.3 us (4%)
  starting transfers between devices  12.8 us (2%)
    another operation x1, loops' own time, entering(): return lax.fori_loop(0, count - 1, turn, total)  157 us
    psum x1, blocking collectives, body(): grad_mix = lax.psum(grad_mix, ('dp', 'seq'))  101 us
    psum x1, waiting for transfers between devices, body(): lax.psum(jnp.concatenate([proj_part, out_part], 1).astype(jnp.bfloat16),...  71 us
    dynamic_slice x62, local copies, waits for them, and re-layouts, turn(): longer = join(total, jax.tree.map(lambda part: part[position], pieces))  39.3 us
    eq x31, other arithmetic, combine(): joined = jnp.where((whole_b == 1) & same, total_a + total_b, total_b)  20.3 us
    unnamed x1, blocking collectives  16.6 us
    ppermute x6, starting transfers between devices, shifted(): return lax.ppermute(array, axis, pairs)  12.7 us
  transfers between devices with their start and end apart: 8, of which 1 were waited for; matrix products, arithmetic and copies ran while one was open for 27% of the time, Pallas kernels for 0%

commit v1 on v0

--- a/solution.py
+++ b/solution.py
@@ -287,7 +287,7 @@
     grad_mix = jnp.einsum(
         "ehf,ef->hf", grad_qtime[:, :, :freq_count], cosines, precision=HIGH
     ) + jnp.einsum("ehf,ef->hf", grad_qtime[:, :, freq_count:], sines, precision=HIGH)
-    grad_mix = lax.psum(grad_mix, ("dp", "seq"))
+    grad_mix = lax.psum(lax.psum(grad_mix, "dp"), "seq")
     factor = float(lax.axis_size("dp") * seq_devices * count) ** (-0.5)
     grad_proj = shard[:, : 4 * model_width] * factor
     grad_out_weight = shard[:, 4 * model_width :] * factor

time: 559 us -> 569 us (1.018)
  loops' own time: 158 us -> 165 us
    another operation x1, loops' own time: 157 us -> 165 us  [entering(): return lax.fori_loop(0, count - 1, turn, total)]
    psum x1 -> x2, blocking collectives: 101 us -> 100 us  [body(): grad_mix = lax.psum(lax.psum(grad_mix, 'dp'), 'seq')]
  transfers between devices with their start and end apart: 8 -> 8, of which waited for: 1 -> 2; matrix products, arithmetic and copies ran while one was open for 27% -> 27% of each run, Pallas kernels for 0% -> 0%
where the time goes in v1:
time: 569 us; the launch traced here: 565 us
  loops' own time  165 us (29%)
  blocking collectives  117 us (21%)
  local copies, waits for them, and re-layouts  83.6 us (15%)
  waiting for transfers between devices  72.5 us (13%)
  other arithmetic  51.7 us (9%)
  matrix products  42.1 us (7%)
  between operations  20.4 us (4%)
  starting transfers between devices  12.8 us (2%)
    another operation x1, loops' own time, entering(): return lax.fori_loop(0, count - 1, turn, total)  165 us
    psum x2, blocking collectives, body(): grad_mix = lax.psum(lax.psum(grad_mix, 'dp'), 'seq')  100 us
    psum x1, waiting for transfers between devices, body(): lax.psum(jnp.concatenate([proj_part, out_part], 1).astype(jnp.bfloat16),...  71.1 us
    dynamic_slice x62, local copies, waits for them, and re-layouts, turn(): longer = join(total, jax.tree.map(lambda part: part[position], pieces))  41.1 us
    eq x31, other arithmetic, combine(): joined = jnp.where((whole_b == 1) & same, total_a + total_b, total_b)  20.4 us
    unnamed x1, blocking collectives  16.6 us
    ppermute x6, starting transfers between devices, shifted(): return lax.ppermute(array, axis, pairs)  12.7 us
  transfers between devices with their start and end apart: 8, of which 2 were waited for; matrix products, arithmetic and copies ran while one was open for 27% of the time, Pallas kernels for 0%

profile of v1, /device:TPU:32, one launch (start us, length us, event | category | flops | bytes accessed | tf_op | source)
XLA Modules:
  0.0 564.6 jit_solution(4729112813480760907)
XLA Ops:
  8.1 2.3 collective-permute-start
  16.5 3.6 gather_fusion.1
  20.1 3.5 gather_fusion
  27.8 16.6 %all-reduce.4 = (s32[32]{0:T(128)S(1)}, s32[32]{0:T(128)S(1)}, s32[32]{0:T(128)S(1)}, s32[32]{0:T(128)S(1)}) all-reduce(s32[32]{0:T(128)S(1)} %dynamic-update-slice, s32[32]{0:T(128)S(1)} %bitcast_dynamic-update-slice_fusion.1, s32[32]{0:T(128)S(1)} %bitcast_dynamic-update-slice_fusion, ...), channel_id=1, replica_groups=mesh['dp'=8,'seq'=32] {'seq'}, use_global_device_ids=true, to_apply=%add | all-reduce | flops 128 | bytes 1024
  44.4 226.1 %while.17 = (s32[]{:T(128)}, s32[1]{0:T(128)}, s32[1]{0:T(128)}, s32[1]{0:T(128)}, s32[]{:T(128)}, /*index=5*/s32[32,1]{0,1:T(1,128)S(1)}, s32[32,1]{0,1:T(1,128...) while((s32[]{:T(128)}, s32[1]{0:T(128)}, s32[1]{0:T(128)}, s32[1]{0:T(128)}, ...), condition=%wide.region_6.7_spmd, body=%wide.region_5.6_spmd.sunk | while | flops 18 | bytes 315 | solution.py:23
  274.8 3.6 multiply_convert_fusion
  280.9 3.8 collective-permute-start.3
  284.8 2.1 collective-permute-start.1
  288.8 2.0 reshape.538
  290.8 2.0 reshape.537
  297.7 10.0 %conditional.5 = (f32[512,4,128]{2,0,1:T(8,128)}) conditional(s32[]{:T(128)} %bitcast.54, () %tuple.57, (bf16[512]{0:T(512)(128)(2,1)S(1)}, s32[512]{0:T(512)S(1)}, bf16[512,4,128]{2,1,0:T(4,128)(2,1)S(1)}, bf16[512,4,128]{2,1,0:T(4,128)(2,1)}, bf16[512,128]{1,0:T(8,128)(2,1)S(1)}, /*index=5*/bf16[512,4,128]{2,0,1:T(8,128)(2,1)S(1)}, ...), branch_computations={%region_9.10_spmd, %region_10.11_spmd} | conditional | flops 815268352 | bytes 12195848 | solution.py:226
  298.8 3.7 fusion.14
  302.5 5.2 fusion.12
  312.2 2.0 reshape.532
  317.0 2.0 multiply_reduce_fusion
  319.0 2.8 multiply_convert_fusion.1
  321.7 2.0 reshape.540
  328.4 29.8 %conditional.6 = (f32[512,4,128]{2,0,1:T(8,128)}, f32[512,4,128]{2,0,1:T(8,128)}, f32[512,512]{1,0:T(8,128)}, f32[512,512]{1,0:T(8,128)}) conditional(s32[]{:T(128)} %bitcast.54, () %tuple.59, (bf16[512]{0:T(512)(128)(2,1)S(1)}, s32[512]{0:T(512)S(1)}, bf16[512,4,128]{2,1,0:T(4,128)(2,1)}, bf16[512,4,128]{2,1,0:T(4,128)(2,1)}, ...), branch_computations={%region_13.14_spmd, %region_14.15_spmd} | conditional | flops 1900020224 | bytes 65018056 | solution.py:250
  332.1 2.1 fusion.26
  335.2 2.4 fusion.22
  337.6 4.3 select_convert_fusion.3
  341.9 2.5 copy.107
  344.4 3.5 fusion.23
  348.0 2.5 copy.53
  350.5 2.6 copy.109
  353.1 3.4 fusion.24
  374.0 17.9 %psum.22 = f32[4,64]{1,0:T(4,128)S(1)} all-reduce(f32[4,64]{1,0:T(4,128)S(1)} %add_bitcast_fusion.3), channel_id=1, replica_groups=mesh['dp'=8,'seq'=32] {'dp'}, use_global_device_ids=true, to_apply=%region_20.21 | all-reduce | flops 256 | bytes 2048 | tf_op jit(solution)/shard_map/psum | solution.py:290
  391.9 82.1 %psum.23 = f32[4,64]{1,0:T(4,128)S(1)} all-reduce(f32[4,64]{1,0:T(4,128)S(1)} %psum.22), channel_id=1, replica_groups=mesh['dp'=8,'seq'=32] {'seq'}, use_global_device_ids=true, to_apply=%region_21.22 | all-reduce | flops 256 | bytes 2048 | tf_op jit(solution)/shard_map/psum | solution.py:290
  474.0 2.3 fusion.54
  476.9 3.9 fusion.56
  482.2 2.3 fusion.67
  484.5 71.1 %all-reduce.7.cloned.1.call-done = bf16[16,2560]{1,0:T(8,128)(2,1)} async-done(((bf16[16,2560]{1,0:T(8,128)(2,1)}), bf16[16,2560]{1,0:T(8,128)(2,1)}) %all-reduce.7.cloned.1.call-update) | async-done | bytes 81936 | tf_op jit(solution)/shard_map/psum | solution.py:285
  (225 shorter events, 120.6 us)
Async XLA Ops:
  7.2 267.6 %copy-start = (bf16[512,2048]{1,0:T(8,128)(2,1)S(1)}, bf16[512,2048]{1,0:T(8,128)(2,1)}, u32[]{:S(2)}) copy-start(bf16[512,2048]{1,0:T(8,128)(2,1)} %param.21) | copy-start | bytes 6291460
  7.2 16.4 %copy-start.23 = (u32[256]{0:T(256)S(1)}, u32[256]{0:T(256)}, u32[]{:S(2)}) copy-start(u32[256]{0:T(256)} %constant.130) | copy-start | bytes 3076
  7.2 263.4 %copy-start.20 = (s32[1,512]{1,0:T(1,128)S(1)}, s32[1,512]{1,0:T(1,128)}, u32[]{:S(2)}) copy-start(s32[1,512]{1,0:T(1,128)} %param.19) | copy-start | bytes 6148
  7.2 263.4 %copy-start.22 = (f32[64]{0:T(128)S(1)}, f32[64]{0:T(128)}, u32[]{:S(2)}) copy-start(f32[64]{0:T(128)} %param.23) | copy-start | bytes 772
  7.2 267.3 %copy-start.5 = (bf16[1,512,512]{2,1,0:T(8,128)(2,1)S(1)}, bf16[1,512,512]{2,1,0:T(8,128)(2,1)}, u32[]{:S(2)}) copy-start(bf16[1,512,512]{2,1,0:T(8,128)(2,1)} %param.18) | copy-start | bytes 1572868
  7.2 474.9 %reduce-scatter.2.cloned.1.call-start = ((), (), s32[]{:S(2)}) async-start(), calls=%async_computation.1 | async-start | bytes 2703360 | tf_op jit(solution)/shard_map/reduce_scatter | solution.py:286
  8.1 299.6 %collective-permute-start = (bf16[512]{0:T(512)(128)(2,1)S(1)}, bf16[512]{0:T(512)(128)(2,1)}, u32[]{:S(2)}, u32[]{:S(2)}) collective-permute-start(bf16[512]{0:T(512)(128)(2,1)S(1)} %convert_reduce_fusion), channel_id=1, source_target_pairs={{0,1},{1,2},{2,3},{3,4},{4,5},{5,6},{6,7},{7,8},{8,9},{9,10},{10,1... | collective-permute-start | bytes 3080 | tf_op jit(solution)/shard_map/ppermute | solution.py:29
  272.6 41.6 %collective-permute-start.2 = (bf16[512,128]{1,0:T(8,128)(2,1)S(1)}, bf16[512,128]{1,0:T(8,128)(2,1)}, u32[]{:S(2)}, u32[]{:S(2)}) collective-permute-start(bf16[512,128]{1,0:T(8,128)(2,1)S(1)} %pad_maximum_fusion.2), channel_id=1, source_target_pairs={{0,1},{1,2},{2,3},{3,4},{4,5},{5,6},{6,7},{7,8},{8,9},{9,10},{10,1... | collective-permute-start | bytes 393224 | tf_op jit(solution)/shard_map/ppermute | solution.py:29
  274.8 12.1 %copy-start.21 = (f32[4,64]{1,0:T(4,128)S(1)}, f32[4,64]{1,0:T(4,128)}, u32[]{:S(2)}) copy-start(f32[4,64]{1,0:T(4,128)} %param.24) | copy-start | bytes 3076
  278.4 1.4 copy-start.11
  280.9 29.4 %collective-permute-start.3 = (bf16[512,512]{1,0:T(8,128)(2,1)}, bf16[512,512]{1,0:T(8,128)(2,1)}, u32[]{:S(2)}, u32[]{:S(2)}) collective-permute-start(bf16[512,512]{1,0:T(8,128)(2,1)} %get-tuple-element.395), channel_id=1, source_target_pairs={{0,1},{1,2},{2,3},{3,4},{4,5},{5,6},{6,7},{7,8},{8,9},{9,10},{10,1... | collective-permute-start | bytes 1572872 | tf_op jit(solution)/shard_map/ppermute | solution.py:29
  284.8 27.5 %collective-permute-start.1 = (bf16[512,512]{1,0:T(8,128)(2,1)}, bf16[512,512]{1,0:T(8,128)(2,1)}, u32[]{:S(2)}, u32[]{:S(2)}) collective-permute-start(bf16[512,512]{1,0:T(8,128)(2,1)} %get-tuple-element.396), channel_id=1, source_target_pairs={{0,1},{1,2},{2,3},{3,4},{4,5},{5,6},{6,7},{7,8},{8,9},{9,10},{10,1... | collective-permute-start | bytes 1572872 | tf_op jit(solution)/shard_map/ppermute | solution.py:29
  324.0 4.4 copy-start.7
  324.0 4.4 copy-start.8
  325.8 37.5 %collective-permute-start.5 = (bf16[512,512]{1,0:T(8,128)(2,1)}, bf16[512,512]{1,0:T(8,128)(2,1)}, u32[]{:S(2)}, u32[]{:S(2)}) collective-permute-start(bf16[512,512]{1,0:T(8,128)(2,1)} %copy_bitcast_fusion.1), channel_id=1, source_target_pairs={{1,0},{2,1},{3,2},{4,3},{5,4},{6,5},{7,6},{8,7},{9,8},{10,9},{11,1... | collective-permute-start | bytes 1572872 | tf_op jit(solution)/shard_map/ppermute | solution.py:29
  327.1 34.6 %collective-permute-start.4 = (bf16[512,512]{1,0:T(8,128)(2,1)}, bf16[512,512]{1,0:T(8,128)(2,1)}, u32[]{:S(2)}, u32[]{:S(2)}) collective-permute-start(bf16[512,512]{1,0:T(8,128)(2,1)} %copy_bitcast_fusion.2), channel_id=1, source_target_pairs={{1,0},{2,1},{3,2},{4,3},{5,4},{6,5},{7,6},{8,7},{9,8},{10,9},{11,1... | collective-permute-start | bytes 1572872 | tf_op jit(solution)/shard_map/ppermute | solution.py:29
  332.1 2.9 copy-start.18
  334.3 1.0 copy-start.19
  335.2 2.4 copy-start.16
  337.6 6.8 %copy-start.4 = (bf16[512,4,128]{0,2,1:T(8,128)(2,1)S(1)}, bf16[512,4,128]{0,2,1:T(8,128)(2,1)}, u32[]{:S(2)}) copy-start(bf16[512,4,128]{0,2,1:T(8,128)(2,1)} %copy.68) | copy-start | bytes 1572868 | tf_op jit(solution)/shard_map/cond
  344.4 8.6 %copy-start.2 = (bf16[512,4,128]{2,1,0:T(4,128)(2,1)S(1)}, bf16[512,4,128]{2,1,0:T(4,128)(2,1)}, u32[]{:S(2)}) copy-start(bf16[512,4,128]{2,1,0:T(4,128)(2,1)} %get-tuple-element.349) | copy-start | bytes 1572868 | tf_op jit(solution)/shard_map/cond
  353.1 3.4 copy-start.1
  359.9 4.9 copy-start.9
  359.9 4.9 copy-start.10
  364.9 2.9 copy-start.6
  366.4 1.3 copy-start.12
  370.9 103.2 %copy-start.15 = (bf16[512,512]{1,0:T(8,128)(2,1)S(1)}, bf16[512,512]{1,0:T(8,128)(2,1)}, u32[]{:S(2)}) copy-start(bf16[512,512]{1,0:T(8,128)(2,1)} %param.22) | copy-start | bytes 1572868
  370.9 184.7 %all-reduce.7.cloned.1.call-start = ((), (), s32[]{:S(2)}) async-start(), calls=%async_computation.2 | async-start | bytes 163840 | tf_op jit(solution)/shard_map/psum | solution.py:285
  476.3 5.9 %copy-start.13 = (bf16[1,512,512]{2,1,0:T(8,128)(2,1)S(1)}, bf16[1,512,512]{2,1,0:T(8,128)(2,1)}, u32[]{:S(2)}) copy-start(bf16[1,512,512]{2,1,0:T(8,128)(2,1)} %param.25) | copy-start | bytes 1572868
Sparse Core Ops, SparseCore 0:
  371.0 111.0 reduce-scatter.1
  484.5 71.0 all-reduce.6
